TPU v7x, 32 devices: a whole 2x2x4 slice. The times are simulated.
32 devices in a mesh: leaf: 4 (over z), row: 2 (over y), col: 4 (over x, core).
Axes of the slice: x: 2, y: 2, z: 4, core: 2. Of those that a mesh axis runs over, the one named last changes fastest.
Arguments:
- rhs_root: bfloat16 [64, 4, 768], P('col', None, ('leaf', 'row')), may hold values from -6 to 6
- rhs_child: bfloat16 [64, 4, 768], P('col', None, ('leaf', 'row')), may hold values from -6 to 6
- subtree_update: bfloat16 [64, 4, 1024], P('col', None, ('leaf', 'row')), may hold values from -6 to 6
- inv_root: bfloat16 [4, 768, 3072], P(None, ('leaf', 'row'), 'col'), as said below
- inv_child: bfloat16 [4, 768, 1536], P(None, ('leaf', 'row'), 'col'), as said below
- off_child: bfloat16 [4, 1024, 1536], P(None, ('leaf', 'row'), 'col'), may hold values from -0.15625 to 0.15625
- child_map: int32 [2, 16], replicated, may hold values from 0 to 23, as said below
- subtree_map: int32 [4, 8], replicated, may hold values from 0 to 27, as said below
Outputs:
- solution_root: float32 [64, 4, 768], P('col', None, ('leaf', 'row'))
- solution_child: float32 [64, 4, 768], P('col', None, ('leaf', 'row'))
- leaf_solution: bfloat16 [64, 4, 1024], P('col', None, ('leaf', 'row'))
Inputs may be any that keep to these rules, and one draw needn't show every extreme that they name: `child_map`: each row names 16 different blocks. `subtree_map`: each row names 8 different blocks. `inv_root`: zero above the diagonal, positive on it. `inv_child`: each child's block is zero above the diagonal, positive on it.
All inputs are finite; a program needn't handle non-finite values.
Results may differ from a plain program's by a relative error of at most 0.017.
Values may be sent and summed in bfloat16 or wider, within the bound.
A program may use at most 64 MiB of HBM per device.

v0:
```python
import jax
import jax.numpy as jnp
from jax import lax
from jax.sharding import PartitionSpec as P

BLOCK_ROWS = 128


def partner_2(block, axis, bit):
    count = lax.axis_size(axis)
    route = []
    for low in range(count):
        high = low | 1 << bit
        if high != low and high < count:
            route += [(low, high), (high, low)]
    return lax.ppermute(block, axis, route)


def group_gather(piece, group_size):
    merged = lax.all_gather(piece, "row", axis=2, tiled=True)
    leaf_index = lax.axis_index("leaf")
    for bit_number in range(group_size.bit_length() - 1):
        partner = partner_2(merged, "leaf", bit_number)
        upper = leaf_index >> bit_number & 1 == 1
        merged = jnp.where(
            upper, jnp.concatenate([partner, merged], 2), jnp.concatenate([merged, partner], 2)
        )
    return merged


def group_sum(partial_sum, group_size):
    leaf_index = lax.axis_index("leaf")
    for bit_number in reversed(range(group_size.bit_length() - 1)):
        middle = partial_sum.shape[1] // 2
        lower_half = partial_sum[:, :middle]
        upper_half = partial_sum[:, middle:]
        upper = leaf_index >> bit_number & 1 == 1
        outgoing = jnp.where(upper, lower_half, upper_half)
        kept_half = jnp.where(upper, upper_half, lower_half)
        partial_sum = kept_half + partner_2(
            outgoing.astype(jnp.bfloat16), "leaf", bit_number
        ).astype(outgoing.dtype)
    return lax.psum_scatter(
        partial_sum.astype(jnp.bfloat16), "row", scatter_dimension=1, tiled=True
    ).astype(jnp.float32)


def one_hot(block_map, blocks_total):
    return (block_map[..., None] == jnp.arange(blocks_total, dtype=jnp.int32)).astype(jnp.bfloat16)


def pick_piece(source, position, along):
    return lax.dynamic_index_in_dim(source, position, along, keepdims=False)


def contract(left_side, right_side, left_dim, right_dim):
    return lax.dot_general(
        left_side,
        right_side,
        (((left_dim,), (right_dim,)), ((), ())),
        preferred_element_type=jnp.float32,
    )


def local(
    rhs_root, rhs_child, subtree_update, inv_root, inv_child, off_child, child_map, subtree_map
):
    n_col = lax.axis_size("col")
    n_row = lax.axis_size("row")
    n_leaf = lax.axis_size("leaf")
    group_size = n_leaf // 2
    sub_size = n_leaf // 4
    col_index = lax.axis_index("col")
    leaf_index = lax.axis_index("leaf")
    row_index = lax.axis_index("row")
    front_index = leaf_index // group_size
    member = leaf_index % group_size
    child_rank = member * n_row + row_index
    half_index = member // sub_size
    sub_rank = member % sub_size * n_row + row_index
    panel_width = rhs_child.shape[0]
    right_sides = panel_width * n_col
    sep_piece = rhs_child.shape[2]
    upd_piece = subtree_update.shape[2]
    root_width = inv_root.shape[2]
    child_width = inv_child.shape[2]
    child_order = child_width * n_col
    child_update = upd_piece * n_col * group_size * n_row
    root_blocks = root_width * n_col // BLOCK_ROWS
    child_blocks = (child_order + child_update) // BLOCK_ROWS
    root_matrix = inv_root.reshape(n_col * sep_piece, root_width)
    child_matrix = inv_child.reshape(n_col * sep_piece, child_width)
    off_matrix = off_child.reshape(n_col * upd_piece, child_width)
    joined = jnp.concatenate([subtree_update, rhs_child], 2)
    gathered = group_gather(joined, group_size).reshape(
        panel_width, n_col, group_size * n_row, upd_piece + sep_piece
    )
    sub_vectors = (
        gathered[..., :upd_piece]
        .reshape(panel_width, n_col, 2, -1)
        .transpose(2, 0, 1, 3)
        .reshape(2, panel_width, -1, BLOCK_ROWS)
    )
    child_rhs_full = gathered[..., upd_piece:].reshape(panel_width, child_order)
    sub_rows = lax.dynamic_slice_in_dim(subtree_map, 2 * front_index, 2, 0)
    spread = jnp.einsum(
        "hpjt,hjn->pnt",
        sub_vectors,
        one_hot(sub_rows, child_blocks),
        preferred_element_type=jnp.float32,
    ).reshape(panel_width, -1)
    child_sep = (spread[:, :child_order] + child_rhs_full.astype(jnp.float32)).astype(jnp.bfloat16)
    child_tail = spread[:, child_order:]
    child_tile = lax.all_to_all(
        child_sep.reshape(panel_width, n_col, child_width),
        "col",
        split_axis=1,
        concat_axis=0,
        tiled=True,
    ).reshape(right_sides, child_width)
    child_forward = lax.psum(contract(child_tile, child_matrix, 1, 1), "col").astype(jnp.bfloat16)
    forward_quarter = lax.dynamic_slice_in_dim(
        child_forward.reshape(right_sides, n_col, sep_piece), col_index, 1, 1
    )
    forward_tile = group_gather(forward_quarter, group_size).reshape(right_sides, child_width)
    pass_term = lax.psum_scatter(
        contract(forward_tile, off_matrix, 1, 1), "col", scatter_dimension=0, tiled=True
    )
    tail_mine = pick_piece(
        child_tail.reshape(panel_width, n_col, group_size * n_row, upd_piece), child_rank, 2
    )
    child_pass = (tail_mine - pass_term.reshape(panel_width, n_col, upd_piece)).astype(jnp.bfloat16)
    joined_root = jnp.concatenate([child_pass, rhs_root], 2)
    root_all = lax.all_gather(joined_root, ("leaf", "row"), axis=2, tiled=True).reshape(
        panel_width, n_col, n_leaf * n_row, upd_piece + sep_piece
    )
    pass_vectors = (
        root_all[..., :upd_piece]
        .reshape(panel_width, n_col, 2, -1)
        .transpose(2, 0, 1, 3)
        .reshape(2, panel_width, -1, BLOCK_ROWS)
    )
    root_rhs_full = root_all[..., upd_piece:].reshape(panel_width, root_width * n_col)
    root_spread = jnp.einsum(
        "hpjt,hjn->pnt",
        pass_vectors,
        one_hot(child_map, root_blocks),
        preferred_element_type=jnp.float32,
    ).reshape(panel_width, -1)
    root_sep = (root_spread + root_rhs_full.astype(jnp.float32)).astype(jnp.bfloat16)
    root_tile = lax.all_to_all(
        root_sep.reshape(panel_width, n_col, root_width),
        "col",
        split_axis=1,
        concat_axis=0,
        tiled=True,
    ).reshape(right_sides, root_width)
    root_forward = lax.psum(contract(root_tile, root_matrix, 1, 1), "col").astype(jnp.bfloat16)
    map_row = pick_piece(child_map, front_index, 0)
    root_piece = lax.psum_scatter(
        contract(root_matrix, root_forward, 0, 1), ("leaf", "row"), scatter_dimension=0, tiled=True
    )
    solution_root = lax.all_to_all(
        root_piece.T.reshape(right_sides, 1, sep_piece),
        "col",
        split_axis=0,
        concat_axis=1,
        tiled=True,
    )
    root_everywhere = lax.all_gather(
        solution_root.astype(jnp.bfloat16), ("leaf", "row"), axis=2, tiled=True
    ).reshape(panel_width, root_blocks, BLOCK_ROWS)
    known_full = (
        jnp.einsum(
            "pnt,jn->pjt",
            root_everywhere,
            one_hot(map_row, root_blocks),
            preferred_element_type=jnp.float32,
        )
        .astype(jnp.bfloat16)
        .reshape(panel_width, child_update)
    )
    known_mine = pick_piece(
        known_full.reshape(panel_width, n_col, group_size * n_row, upd_piece), child_rank, 2
    )
    known_rows = lax.all_gather(known_mine, "col", axis=0, tiled=True).reshape(
        right_sides, n_col * upd_piece
    )
    correction = group_sum(contract(known_rows, off_matrix, 1, 0), group_size)
    back_quarter = (
        forward_quarter.reshape(right_sides, sep_piece).astype(jnp.float32) - correction
    ).astype(jnp.bfloat16)
    back_rows = lax.all_gather(
        back_quarter.reshape(right_sides, 1, sep_piece), "col", axis=1, tiled=True
    ).reshape(right_sides, n_col * sep_piece)
    child_piece = group_sum(contract(back_rows, child_matrix, 1, 0), group_size)
    solution_child = lax.all_to_all(
        child_piece.reshape(right_sides, 1, sep_piece),
        "col",
        split_axis=0,
        concat_axis=1,
        tiled=True,
    )
    child_rounded = solution_child.astype(jnp.bfloat16)
    sep_whole = group_gather(child_rounded, group_size).reshape(panel_width, child_order)
    child_whole = jnp.concatenate([sep_whole, known_full], 1)
    sub_row = pick_piece(subtree_map, 2 * front_index + half_index, 0)
    leaf_full = jnp.einsum(
        "pnt,jn->pjt",
        child_whole.reshape(panel_width, child_blocks, BLOCK_ROWS),
        one_hot(sub_row, child_blocks),
        preferred_element_type=jnp.float32,
    ).astype(jnp.bfloat16)
    leaf_solution = pick_piece(
        leaf_full.reshape(panel_width, n_col, sub_size * n_row, upd_piece), sub_rank, 2
    )
    return (solution_root, solution_child, leaf_solution)


def solution(mesh):
    in_specs = (
        P("col", None, ("leaf", "row")),
        P("col", None, ("leaf", "row")),
        P("col", None, ("leaf", "row")),
        P(None, ("leaf", "row"), "col"),
        P(None, ("leaf", "row"), "col"),
        P(None, ("leaf", "row"), "col"),
        P(),
        P(),
    )
    out_specs = (
        P("col", None, ("leaf", "row")),
        P("col", None, ("leaf", "row")),
        P("col", None, ("leaf", "row")),
    )
    return jax.shard_map(local, mesh=mesh, in_specs=in_specs, out_specs=out_specs, check_vma=False)
```

profile of v0, /device:TPU:0, one launch (start us, length us, event | category | flops | bytes accessed | tf_op | source)
XLA Modules:
  0.0 315.4 jit_solution(6186895764628182573)
XLA Ops:
  7.2 0.9 copy.131
  9.2 9.2 %all_gather.21 = bf16[16,4,448]{0,1,2:T(4,128)(2,1)S(1)} all-gather(bf16[16,4,224]{0,1,2:T(4,128)(2,1)S(1)} %pad_maximum_fusion), channel_id=1, replica_groups=mesh['leaf'=4,'row'=2,'col'=4] {'row'}, dimensions={2}, use_global_device_ids=true | all-gather | bytes 86016 | tf_op jit(solution)/shard_map/all_gather | solution.py:20
  18.4 1.8 collective-permute-start
  20.6 9.6 %collective-permute-done = bf16[16,4,448]{0,1,2:T(4,128)(2,1)S(1)} collective-permute-done((bf16[16,4,448]{0,1,2:T(4,128)(2,1)S(1)}, bf16[16,4,448]{0,1,2:T(4,128)(2,1)S(1)}, u32[]{:S(2)}, u32[]{:S(2)}) %collective-permute-start) | collective-permute-done | bytes 57376 | tf_op jit(solution)/shard_map/ppermute | solution.py:16
  32.2 3.3 %all-to-all-start = ((bf16[16,4,384]{2,0,1:T(8,128)(2,1)}), bf16[16,4,384]{2,0,1:T(8,128)(2,1)S(1)}, u32[]{:S(2)}, u32[]{:S(2)}) async-start(bf16[16,4,384]{2,0,1:T(8,128)(2,1)} %bitcast.141), calls=%async_computation | async-start | bytes 98304 | tf_op jit(solution)/shard_map/all_to_all | solution.py:114
  35.5 3.9 %all-to-all-done = bf16[16,4,384]{2,0,1:T(8,128)(2,1)S(1)} async-done(((bf16[16,4,384]{2,0,1:T(8,128)(2,1)}), bf16[16,4,384]{2,0,1:T(8,128)(2,1)S(1)}, u32[]{:S(2)}, u32[]{:S(2)}) %all-to-all-start) | async-done | bytes 49184 | tf_op jit(solution)/shard_map/all_to_all | solution.py:114
  39.7 11.1 %psum.14 = bf16[64,384]{1,0:T(8,128)(2,1)S(1)} all-reduce(f32[64,384]{1,0:T(8,128)S(1)} %fusion.31), channel_id=1, replica_groups=mesh['leaf'=4,'row'=2,'col'=4] {'col'}, use_global_device_ids=true, to_apply=%region_0.1 | all-reduce | flops 24576 | bytes 147456 | tf_op jit(solution)/shard_map/psum | solution.py:121
  51.1 4.8 %all_gather.22 = bf16[64,1,192]{0,1,2:T(2,128)(2,1)S(1)} all-gather(bf16[64,1,96]{0,1,2:T(2,128)(2,1)S(1)} %copy.178), channel_id=1, replica_groups=mesh['leaf'=4,'row'=2,'col'=4] {'row'}, dimensions={2}, use_global_device_ids=true | all-gather | bytes 36864 | tf_op jit(solution)/shard_map/all_gather | solution.py:20
  55.9 1.6 collective-permute-start.1
  57.5 2.4 collective-permute-done.1
  61.4 20.5 %reduce-scatter.11.cloned.1.call-done = f32[16,512]{1,0:T(8,128)} async-done(((f32[64,512]{1,0:T(8,128)}), f32[16,512]{1,0:T(8,128)}) %reduce-scatter.11.cloned.1.call-update) | async-done | bytes 32784 | tf_op jit(solution)/shard_map/reduce_scatter | solution.py:126
  83.1 41.1 %all_gather.23 = bf16[16,4,1792]{0,1,2:T(4,128)(2,1)S(1)} all-gather(bf16[16,4,224]{0,1,2:T(4,128)(2,1)S(1)} %pad_maximum_fusion.1), channel_id=1, replica_groups=mesh['leaf'=4,'row'=2,'col'=4] {'leaf','row'}, dimensions={2}, use_global_device_ids=true | all-gather | bytes 258048 | tf_op jit(solution)/shard_map/all_gather | solution.py:134
  126.7 6.7 %all_to_all.66 = bf16[16,4,768]{2,0,1:T(8,128)(2,1)S(1)} all-to-all(bf16[16,4,768]{2,0,1:T(8,128)(2,1)S(1)} %fusion.1), channel_id=1, replica_groups=mesh['leaf'=4,'row'=2,'col'=4] {'col'}, dimensions={1} | all-to-all | bytes 196608 | tf_op jit(solution)/shard_map/all_to_all | solution.py:151
  133.7 11.2 %psum.15 = bf16[64,384]{1,0:T(8,128)(2,1)S(1)} all-reduce(f32[64,384]{1,0:T(8,128)S(1)} %fusion.32), channel_id=1, replica_groups=mesh['leaf'=4,'row'=2,'col'=4] {'col'}, use_global_device_ids=true, to_apply=%region_2.3 | all-reduce | flops 24576 | bytes 147456 | tf_op jit(solution)/shard_map/psum | solution.py:158
  145.0 0.9 copy.172
  146.0 60.1 %reduce-scatter.13.cloned.1.call-done = f32[96,64]{1,0:T(8,128)} async-done(((f32[768,64]{1,0:T(8,128)}), f32[96,64]{1,0:T(8,128)}) %reduce-scatter.13.cloned.1.call-update) | async-done | bytes 24592
  206.1 1.5 copy.173
  207.6 3.3 %all-to-all-start.2 = ((f32[64,1,96]{2,1,0:T(1,128)}), f32[64,1,96]{2,1,0:T(1,128)S(1)}, u32[]{:S(2)}, u32[]{:S(2)}) async-start(f32[64,1,96]{2,1,0:T(1,128)} %bitcast.28), calls=%async_computation.3 | async-start | bytes 65536 | tf_op jit(solution)/shard_map/all_to_all | solution.py:163
  211.0 3.8 %all-to-all-done.2 = f32[64,1,96]{2,1,0:T(1,128)S(1)} async-done(((f32[64,1,96]{2,1,0:T(1,128)}), f32[64,1,96]{2,1,0:T(1,128)S(1)}, u32[]{:S(2)}, u32[]{:S(2)}) %all-to-all-start.2) | async-done | bytes 24608 | tf_op jit(solution)/shard_map/all_to_all | solution.py:163
  215.0 32.0 %all_gather.24 = bf16[16,4,768]{0,1,2:T(4,128)(2,1)S(1)} all-gather(bf16[16,4,96]{0,1,2:T(4,128)(2,1)S(1)} %bitcast.161), channel_id=1, replica_groups=mesh['leaf'=4,'row'=2,'col'=4] {'leaf','row'}, dimensions={2}, use_global_device_ids=true | all-gather | bytes 110592 | tf_op jit(solution)/shard_map/all_gather | solution.py:170
  247.8 5.2 %all-gather = bf16[64,4,1,128]{3,0,1,2:T(8,128)(2,1)S(1)} all-gather(bf16[16,4,1,128]{3,0,1,2:T(8,128)(2,1)S(1)} %copy.181), channel_id=2, replica_groups=mesh['leaf'=4,'row'=2,'col'=4] {'col'}, dimensions={0}, use_global_device_ids=true | all-gather | bytes 81920 | tf_op jit(solution)/shard_map/all_gather | solution.py:186
  253.4 3.9 %collective-permute-done.2 = bf16[64,192]{1,0:T(8,128)(2,1)S(1)} collective-permute-done((bf16[64,192]{1,0:T(8,128)(2,1)S(1)}, bf16[64,192]{1,0:T(8,128)(2,1)S(1)}, u32[]{:S(2)}, u32[]{:S(2)}) %collective-permute-start.2) | collective-permute-done | bytes 24608 | tf_op jit(solution)/shard_map/ppermute | solution.py:16
  258.3 8.1 %reduce-scatter.15.cloned.1.call-done = bf16[96,64]{1,0:T(8,128)(2,1)} async-done(((bf16[192,64]{1,0:T(8,128)(2,1)}), bf16[96,64]{1,0:T(8,128)(2,1)}) %reduce-scatter.15.cloned.1.call-update) | async-done | bytes 12304
  267.2 5.2 %all-gather.2 = bf16[4,96,64]{1,2,0:T(8,128)(2,1)S(1)} all-gather(bf16[1,96,64]{1,2,0:T(8,128)(2,1)S(1)} %copy.154), channel_id=3, replica_groups=mesh['leaf'=4,'row'=2,'col'=4] {'col'}, dimensions={0}, use_global_device_ids=true | all-gather | bytes 61440 | tf_op jit(solution)/shard_map/all_gather | solution.py:193
  273.1 1.6 collective-permute-start.3
  274.6 2.4 collective-permute-done.3
  277.9 10.0 %reduce-scatter.17.cloned.1.call-done = bf16[96,64]{1,0:T(8,128)(2,1)} async-done(((bf16[192,64]{1,0:T(8,128)(2,1)}), bf16[96,64]{1,0:T(8,128)(2,1)}) %reduce-scatter.17.cloned.1.call-update) | async-done | bytes 12304
  289.3 3.3 %all-to-all-start.3 = ((f32[64,1,96]{2,1,0:T(1,128)}), f32[64,1,96]{2,1,0:T(1,128)S(1)}, u32[]{:S(2)}, u32[]{:S(2)}) async-start(f32[64,1,96]{2,1,0:T(1,128)} %bitcast.46), calls=%async_computation.4 | async-start | bytes 65536 | tf_op jit(solution)/shard_map/all_to_all | solution.py:197
  292.6 3.9 %all-to-all-done.3 = f32[64,1,96]{2,1,0:T(1,128)S(1)} async-done(((f32[64,1,96]{2,1,0:T(1,128)}), f32[64,1,96]{2,1,0:T(1,128)S(1)}, u32[]{:S(2)}, u32[]{:S(2)}) %all-to-all-start.3) | async-done | bytes 24608 | tf_op jit(solution)/shard_map/all_to_all | solution.py:197
  296.7 5.3 %all_gather.27 = bf16[16,4,192]{0,1,2:T(4,128)(2,1)S(1)} all-gather(bf16[16,4,96]{0,1,2:T(4,128)(2,1)S(1)} %bitcast.162), channel_id=1, replica_groups=mesh['leaf'=4,'row'=2,'col'=4] {'row'}, dimensions={2}, use_global_device_ids=true | all-gather | bytes 36864 | tf_op jit(solution)/shard_map/all_gather | solution.py:20
  302.0 1.5 collective-permute-start.4
  304.9 2.8 collective-permute-done.4
  (102 shorter events, 18.1 us)
Async XLA Ops:
  7.2 126.2 %copy-start = (bf16[4,96,768]{2,1,0:T(8,128)(2,1)S(1)}, bf16[4,96,768]{2,1,0:T(8,128)(2,1)}, u32[]{:S(2)}) copy-start(bf16[4,96,768]{2,1,0:T(8,128)(2,1)} %param.11) | copy-start | bytes 1769476
  7.2 13.4 %copy-start.5 = (s32[4,8]{1,0:T(4,128)S(1)}, s32[4,8]{1,0:T(4,128)}, u32[]{:S(2)}) copy-start(s32[4,8]{1,0:T(4,128)} %param.15) | copy-start | bytes 388
  18.4 21.0 %copy-start.2 = (bf16[4,96,384]{2,1,0:T(8,128)(2,1)S(1)}, bf16[4,96,384]{2,1,0:T(8,128)(2,1)}, u32[]{:S(2)}) copy-start(bf16[4,96,384]{2,1,0:T(8,128)(2,1)} %param.12) | copy-start | bytes 884740
  18.4 11.7 %collective-permute-start = (bf16[16,4,448]{0,1,2:T(4,128)(2,1)S(1)}, bf16[16,4,448]{0,1,2:T(4,128)(2,1)S(1)}, u32[]{:S(2)}, u32[]{:S(2)}) collective-permute-start(bf16[16,4,448]{0,1,2:T(4,128)(2,1)S(1)} %all_gather.21), channel_id=1, source_target_pairs={{0,8},{8,0},{16,24},{24,16},{1,9},{9,1},{17,25},{25,17},{2,10},{10... | collective-permute-start | bytes 172040 | tf_op jit(solution)/shard_map/ppermute | solution.py:16
  30.4 29.5 %copy-start.1 = (bf16[4,128,384]{2,1,0:T(8,128)(2,1)S(1)}, bf16[4,128,384]{2,1,0:T(8,128)(2,1)}, u32[]{:S(2)}) copy-start(bf16[4,128,384]{2,1,0:T(8,128)(2,1)} %param.13) | copy-start | bytes 1179652
  30.9 30.0 %copy-start.3 = (bf16[16,4,96]{2,1,0:T(4,128)(2,1)S(1)}, bf16[16,4,96]{2,1,0:T(4,128)(2,1)}, u32[]{:S(2)}) copy-start(bf16[16,4,96]{2,1,0:T(4,128)(2,1)} %param.8) | copy-start | bytes 36868
  32.2 7.3 %all-to-all-start = ((bf16[16,4,384]{2,0,1:T(8,128)(2,1)}), bf16[16,4,384]{2,0,1:T(8,128)(2,1)S(1)}, u32[]{:S(2)}, u32[]{:S(2)}) async-start(bf16[16,4,384]{2,0,1:T(8,128)(2,1)} %bitcast.141), calls=%async_computation | async-start | bytes 98304 | tf_op jit(solution)/shard_map/all_to_all | solution.py:114
  35.4 46.4 %reduce-scatter.11.cloned.1.call-start = ((), (), s32[]{:S(2)}) async-start(), calls=%async_computation.8 | async-start | bytes 163840 | tf_op jit(solution)/shard_map/reduce_scatter | solution.py:126
  55.9 4.0 %collective-permute-start.1 = (bf16[64,1,192]{2,0,1:T(8,128)(2,1)S(1)}, bf16[64,1,192]{2,0,1:T(8,128)(2,1)S(1)}, u32[]{:S(2)}, u32[]{:S(2)}) collective-permute-start(bf16[64,1,192]{2,0,1:T(8,128)(2,1)S(1)} %copy.141), channel_id=1, source_target_pairs={{0,8},{8,0},{16,24},{24,16},{1,9},{9,1},{17,25},{25,17},{2,10},{10... | collective-permute-start | bytes 73736 | tf_op jit(solution)/shard_map/ppermute | solution.py:16
  60.8 145.3 %reduce-scatter.13.cloned.1.call-start = ((), (), s32[]{:S(2)}) async-start(), calls=%async_computation.9 | async-start | bytes 442368
  124.5 1.1 copy-start.4
  207.6 7.2 %all-to-all-start.2 = ((f32[64,1,96]{2,1,0:T(1,128)}), f32[64,1,96]{2,1,0:T(1,128)S(1)}, u32[]{:S(2)}, u32[]{:S(2)}) async-start(f32[64,1,96]{2,1,0:T(1,128)} %bitcast.28), calls=%async_computation.3 | async-start | bytes 65536 | tf_op jit(solution)/shard_map/all_to_all | solution.py:163
  210.9 55.5 %reduce-scatter.15.cloned.1.call-start = ((), (), s32[]{:S(2)}) async-start(), calls=%async_computation.10 | async-start | bytes 73728
  253.4 4.0 %collective-permute-start.2 = (bf16[64,192]{1,0:T(8,128)(2,1)S(1)}, bf16[64,192]{1,0:T(8,128)(2,1)S(1)}, u32[]{:S(2)}, u32[]{:S(2)}) collective-permute-start(bf16[64,192]{1,0:T(8,128)(2,1)S(1)} %select_convert_fusion.1), channel_id=1, source_target_pairs={{0,8},{8,0},{16,24},{24,16},{1,9},{9,1},{17,25},{25,17},{2,10},{10... | collective-permute-start | bytes 73736 | tf_op jit(solution)/shard_map/ppermute | solution.py:16
  258.2 29.7 %reduce-scatter.17.cloned.1.call-start = ((), (), s32[]{:S(2)}) async-start(), calls=%async_computation.11 | async-start | bytes 73728
  273.1 4.0 %collective-permute-start.3 = (bf16[64,192]{1,0:T(8,128)(2,1)S(1)}, bf16[64,192]{1,0:T(8,128)(2,1)S(1)}, u32[]{:S(2)}, u32[]{:S(2)}) collective-permute-start(bf16[64,192]{1,0:T(8,128)(2,1)S(1)} %select_convert_fusion), channel_id=1, source_target_pairs={{0,8},{8,0},{16,24},{24,16},{1,9},{9,1},{17,25},{25,17},{2,10},{10... | collective-permute-start | bytes 73736 | tf_op jit(solution)/shard_map/ppermute | solution.py:16
  289.3 7.2 %all-to-all-start.3 = ((f32[64,1,96]{2,1,0:T(1,128)}), f32[64,1,96]{2,1,0:T(1,128)S(1)}, u32[]{:S(2)}, u32[]{:S(2)}) async-start(f32[64,1,96]{2,1,0:T(1,128)} %bitcast.46), calls=%async_computation.4 | async-start | bytes 65536 | tf_op jit(solution)/shard_map/all_to_all | solution.py:197
  302.0 5.7 %collective-permute-start.4 = (bf16[16,4,192]{0,1,2:T(4,128)(2,1)S(1)}, bf16[16,4,192]{0,1,2:T(4,128)(2,1)S(1)}, u32[]{:S(2)}, u32[]{:S(2)}) collective-permute-start(bf16[16,4,192]{0,1,2:T(4,128)(2,1)S(1)} %all_gather.27), channel_id=1, source_target_pairs={{0,8},{8,0},{16,24},{24,16},{1,9},{9,1},{17,25},{25,17},{2,10},{10... | collective-permute-start | bytes 73736 | tf_op jit(solution)/shard_map/ppermute | solution.py:16
Sparse Core Ops, SparseCore 0:
  60.9 20.8 reduce-scatter.10
  146.1 59.9 reduce-scatter.12
  258.3 8.0 reduce-scatter.14
  278.0 9.8 reduce-scatter.16
where the time goes:
time: 316 us; the launch traced here: 315 us
  blocking collectives  132 us (42%)
  waiting for transfers between devices  132 us (42%)
  starting transfers between devices  16.5 us (5%)
  local copies, waits for them, and re-layouts  15.4 us (5%)
  between operations  14.4 us (5%)
    unnamed x7, waiting for transfers between devices  78.3 us
    all_gather x1, blocking collectives, local(): lax.all_gather(joined_root, ('leaf', 'row'), axis=2, tiled=True)  41.1 us
    all_gather x1, blocking collectives, local(): lax.all_gather(solution_root.astype(jnp.bfloat16), ('leaf', 'row'), axis=...  32 us
    ppermute x5, waiting for transfers between devices, partner_2(): return lax.ppermute(block, axis, route)  21.1 us
    reduce_scatter x1, waiting for transfers between devices, local(): lax.psum_scatter(contract(forward_tile, off_matrix, 1, 1), 'col', scatter...  20.5 us
    all_gather x3, blocking collectives, group_gather(): merged = lax.all_gather(piece, 'row', axis=2, tiled=True)  19.3 us
    psum x1, blocking collectives, local(): lax.psum(contract(root_tile, root_matrix, 1, 1), 'col').astype(jnp.bfloat16)  11.2 us
    psum x1, blocking collectives, local(): lax.psum(contract(child_tile, child_matrix, 1, 1), 'col')  11.1 us
  transfers between devices with their start and end apart: 12, of which 12 were waited for; matrix products, arithmetic and copies ran while one was open for 1% of the time, Pallas kernels for 0%

commit v1 on v0

--- a/solution.py
+++ b/solution.py
@@ -4,6 +4,12 @@
 from jax.sharding import PartitionSpec as P
 
 BLOCK_ROWS = 128
+
+
+def hold_islands(v0, out_dim):
+    k_now = list(v0.shape[1:])
+    k_now[out_dim] *= v0.shape[0]
+    return jnp.moveaxis(v0, 0, out_dim).reshape(k_now)
 
 
 def partner_2(block, axis, bit):
@@ -131,7 +137,25 @@
     )
     child_pass = (tail_mine - pass_term.reshape(panel_width, n_col, upd_piece)).astype(jnp.bfloat16)
     joined_root = jnp.concatenate([child_pass, rhs_root], 2)
-    root_all = lax.all_gather(joined_root, ("leaf", "row"), axis=2, tiled=True).reshape(
+
+    def attach_results(s0, shard_axis, dim_k):
+        n_lanes = lax.psum(1, shard_axis)
+        all_blocks = [(d, (d + 1) % n_lanes) for d in range(n_lanes)]
+        crops = [(to_i, dev) for dev, to_i in all_blocks]
+        moved, lower = ([], [])
+        for s in range(n_lanes - 1):
+            if s % 2 == 0:
+                t1 = lax.ppermute(moved[-1] if moved else s0, shard_axis, perm=all_blocks)
+                moved.append(t1)
+            else:
+                lower.append(lax.ppermute(lower[-1] if lower else s0, shard_axis, crops))
+        after = jnp.stack([*moved[::-1], s0, *lower])
+        block_next = lax.axis_index(shard_axis)
+        e_next = block_next - len(moved)
+        after = after[(jnp.arange(n_lanes) - e_next) % n_lanes]
+        return hold_islands(after, dim_k)
+
+    root_all = attach_results(joined_root, ("leaf", "row"), 2).reshape(
         panel_width, n_col, n_leaf * n_row, upd_piece + sep_piece
     )
     pass_vectors = (

time: 316 us -> 303 us (0.959)
  blocking collectives: 132 us -> 90.9 us
  starting transfers between devices: 16.5 us -> 32.2 us
  waiting for transfers between devices: 132 us -> 144 us
    all_gather x1 -> x0, blocking collectives: 41.1 us -> none  [local(): lax.all_gather(joined_root, ('leaf', 'row'), axis=2, tiled=True)]
    ppermute x0 -> x7, starting transfers between devices: none -> 15.8 us  [the longest x3 14.3 us: attach_results(): lower.append(lax.ppermute(lower[-1] if lower else s0, shard_axis, crops))]
    ppermute x0 -> x7, waiting for transfers between devices: none -> 10.7 us  [the longest x4 10.7 us: attach_results(): t1 = lax.ppermute(moved[-1] if moved else s0, shard_axis, perm=all_blocks)]
    unnamed x29 -> x36, local copies, waits for them, and re-layouts: 8.16 us -> 8.81 us
  transfers between devices with their start and end apart: 12 -> 19, of which waited for: 12 -> 16; matrix products, arithmetic and copies ran while one was open for 1% -> 1% of each run, Pallas kernels for 0% -> 0%
where the time goes in v1:
time: 303 us; the launch traced here: 302 us
  waiting for transfers between devices  144 us (48%)
  blocking collectives  90.9 us (30%)
  starting transfers between devices  32.2 us (11%)
  local copies, waits for them, and re-layouts  14.5 us (5%)
  between operations  14.4 us (5%)
  other arithmetic  3.24 us (1%)
  matrix products  3.06 us (1%)
    unnamed x7, waiting for transfers between devices  80.9 us
    all_gather x1, blocking collectives, local(): lax.all_gather(solution_root.astype(jnp.bfloat16), ('leaf', 'row'), axis=...  32 us
    ppermute x5, waiting for transfers between devices, partner_2(): return lax.ppermute(block, axis, route)  20.4 us
    reduce_scatter x1, waiting for transfers between devices, local(): lax.psum_scatter(contract(forward_tile, off_matrix, 1, 1), 'col', scatter...  20.1 us
    all_gather x3, blocking collectives, group_gather(): merged = lax.all_gather(piece, 'row', axis=2, tiled=True)  19.3 us
    ppermute x3, starting transfers between devices, attach_results(): lower.append(lax.ppermute(lower[-1] if lower else s0, shard_axis, crops))  14.3 us
    psum x1, blocking collectives, local(): lax.psum(contract(child_tile, child_matrix, 1, 1), 'col')  11.2 us
    psum x1, blocking collectives, local(): lax.psum(contract(root_tile, root_matrix, 1, 1), 'col').astype(jnp.bfloat16)  11.2 us
  transfers between devices with their start and end apart: 19, of which 16 were waited for; matrix products, arithmetic and copies ran while one was open for 1% of the time, Pallas kernels for 0%

profile of v1, /device:TPU:0, one launch (start us, length us, event | category | flops | bytes accessed | tf_op | source)
XLA Modules:
  0.0 302.2 jit_solution(2397453470698376762)
XLA Ops:
  8.5 9.2 %all_gather.18 = bf16[16,4,448]{0,1,2:T(4,128)(2,1)S(1)} all-gather(bf16[16,4,224]{0,1,2:T(4,128)(2,1)S(1)} %pad_maximum_fusion), channel_id=1, replica_groups=mesh['leaf'=4,'row'=2,'col'=4] {'row'}, dimensions={2}, use_global_device_ids=true | all-gather | bytes 86016 | tf_op jit(solution)/shard_map/all_gather | solution.py:26
  17.7 1.8 collective-permute-start
  20.5 8.9 %collective-permute-done = bf16[16,4,448]{0,1,2:T(4,128)(2,1)S(1)} collective-permute-done((bf16[16,4,448]{0,1,2:T(4,128)(2,1)S(1)}, bf16[16,4,448]{0,1,2:T(4,128)(2,1)S(1)}, u32[]{:S(2)}, u32[]{:S(2)}) %collective-permute-start) | collective-permute-done | bytes 57376 | tf_op jit(solution)/shard_map/ppermute | solution.py:22
  31.4 3.3 %all-to-all-start = ((bf16[16,4,384]{2,0,1:T(8,128)(2,1)}), bf16[16,4,384]{2,0,1:T(8,128)(2,1)S(1)}, u32[]{:S(2)}, u32[]{:S(2)}) async-start(bf16[16,4,384]{2,0,1:T(8,128)(2,1)} %bitcast.167), calls=%async_computation | async-start | bytes 98304 | tf_op jit(solution)/shard_map/all_to_all | solution.py:120
  34.8 3.9 %all-to-all-done = bf16[16,4,384]{2,0,1:T(8,128)(2,1)S(1)} async-done(((bf16[16,4,384]{2,0,1:T(8,128)(2,1)}), bf16[16,4,384]{2,0,1:T(8,128)(2,1)S(1)}, u32[]{:S(2)}, u32[]{:S(2)}) %all-to-all-start) | async-done | bytes 49184 | tf_op jit(solution)/shard_map/all_to_all | solution.py:120
  38.9 11.2 %psum.14 = bf16[64,384]{1,0:T(8,128)(2,1)S(1)} all-reduce(f32[64,384]{1,0:T(8,128)S(1)} %fusion.33), channel_id=1, replica_groups=mesh['leaf'=4,'row'=2,'col'=4] {'col'}, use_global_device_ids=true, to_apply=%region_0.1 | all-reduce | flops 24576 | bytes 147456 | tf_op jit(solution)/shard_map/psum | solution.py:127
  50.5 4.8 %all_gather.19 = bf16[64,1,192]{0,1,2:T(2,128)(2,1)S(1)} all-gather(bf16[64,1,96]{0,1,2:T(2,128)(2,1)S(1)} %copy.195), channel_id=1, replica_groups=mesh['leaf'=4,'row'=2,'col'=4] {'row'}, dimensions={2}, use_global_device_ids=true | all-gather | bytes 36864 | tf_op jit(solution)/shard_map/all_gather | solution.py:26
  56.9 2.4 collective-permute-done.1
  61.1 20.1 %reduce-scatter.11.cloned.1.call-done = f32[16,512]{1,0:T(8,128)} async-done(((f32[64,512]{1,0:T(8,128)}), f32[16,512]{1,0:T(8,128)}) %reduce-scatter.11.cloned.1.call-update) | async-done | bytes 32784 | tf_op jit(solution)/shard_map/reduce_scatter | solution.py:132
  83.6 5.1 %collective-permute-done.2 = bf16[16,4,224]{2,0,1:T(8,128)(2,1)S(1)} collective-permute-done((bf16[16,4,224]{2,0,1:T(8,128)(2,1)S(1)}, bf16[16,4,224]{2,0,1:T(8,128)(2,1)S(1)}, u32[]{:S(2)}, u32[]{:S(2)}) %collective-permute-start.2) | collective-permute-done | bytes 28704 | tf_op jit(solution)/shard_map/ppermute | solution.py:148
  88.7 4.7 %collective-permute-start.6 = (bf16[16,4,224]{2,0,1:T(8,128)(2,1)S(1)}, bf16[16,4,224]{2,0,1:T(8,128)(2,1)S(1)}, u32[]{:S(2)}, u32[]{:S(2)}) collective-permute-start(bf16[16,4,224]{2,0,1:T(8,128)(2,1)S(1)} %pad_maximum_fusion.2), channel_id=1, source_target_pairs={{4,0},{8,4},{12,8},{16,12},{20,16},{24,20},{28,24},{0,28},{5,1},{9... | collective-permute-start | bytes 86024 | tf_op jit(solution)/shard_map/ppermute | solution.py:151
  93.4 1.9 collective-permute-done.3
  95.4 4.8 %collective-permute-start.7 = (bf16[16,4,224]{2,0,1:T(8,128)(2,1)S(1)}, bf16[16,4,224]{2,0,1:T(8,128)(2,1)S(1)}, u32[]{:S(2)}, u32[]{:S(2)}) collective-permute-start(bf16[16,4,224]{2,0,1:T(8,128)(2,1)S(1)} %collective-permute-done.6), channel_id=1, source_target_pairs={{4,0},{8,4},{12,8},{16,12},{20,16},{24,20},{28,24},{0,28},{5,1},{9... | collective-permute-start | bytes 86024 | tf_op jit(solution)/shard_map/ppermute | solution.py:151
  100.1 1.8 collective-permute-done.4
  102.0 4.8 %collective-permute-start.8 = (bf16[16,4,224]{2,0,1:T(8,128)(2,1)S(1)}, bf16[16,4,224]{2,0,1:T(8,128)(2,1)S(1)}, u32[]{:S(2)}, u32[]{:S(2)}) collective-permute-start(bf16[16,4,224]{2,0,1:T(8,128)(2,1)S(1)} %collective-permute-done.7), channel_id=1, source_target_pairs={{4,0},{8,4},{12,8},{16,12},{20,16},{24,20},{28,24},{0,28},{5,1},{9... | collective-permute-start | bytes 86024 | tf_op jit(solution)/shard_map/ppermute | solution.py:151
  106.8 1.8 collective-permute-done.5
  110.9 6.7 %all_to_all.66 = bf16[16,4,768]{2,0,1:T(8,128)(2,1)S(1)} all-to-all(bf16[16,4,768]{2,0,1:T(8,128)(2,1)S(1)} %fusion), channel_id=1, replica_groups=mesh['leaf'=4,'row'=2,'col'=4] {'col'}, dimensions={1} | all-to-all | bytes 196608 | tf_op jit(solution)/shard_map/all_to_all | solution.py:175
  117.9 11.2 %psum.15 = bf16[64,384]{1,0:T(8,128)(2,1)S(1)} all-reduce(f32[64,384]{1,0:T(8,128)S(1)} %fusion.34), channel_id=1, replica_groups=mesh['leaf'=4,'row'=2,'col'=4] {'col'}, use_global_device_ids=true, to_apply=%region_2.3 | all-reduce | flops 24576 | bytes 147456 | tf_op jit(solution)/shard_map/psum | solution.py:182
  130.2 62.7 %reduce-scatter.13.cloned.1.call-done = f32[96,64]{1,0:T(8,128)} async-done(((f32[768,64]{1,0:T(8,128)}), f32[96,64]{1,0:T(8,128)}) %reduce-scatter.13.cloned.1.call-update) | async-done | bytes 24592
  194.4 3.3 %all-to-all-start.2 = ((f32[64,1,96]{2,1,0:T(1,128)}), f32[64,1,96]{2,1,0:T(1,128)S(1)}, u32[]{:S(2)}, u32[]{:S(2)}) async-start(f32[64,1,96]{2,1,0:T(1,128)} %bitcast.37), calls=%async_computation.3 | async-start | bytes 65536 | tf_op jit(solution)/shard_map/all_to_all | solution.py:187
  197.8 3.8 %all-to-all-done.2 = f32[64,1,96]{2,1,0:T(1,128)S(1)} async-done(((f32[64,1,96]{2,1,0:T(1,128)}), f32[64,1,96]{2,1,0:T(1,128)S(1)}, u32[]{:S(2)}, u32[]{:S(2)}) %all-to-all-start.2) | async-done | bytes 24608 | tf_op jit(solution)/shard_map/all_to_all | solution.py:187
  201.8 32.0 %all_gather.20 = bf16[16,4,768]{0,1,2:T(4,128)(2,1)S(1)} all-gather(bf16[16,4,96]{0,1,2:T(4,128)(2,1)S(1)} %bitcast.186), channel_id=1, replica_groups=mesh['leaf'=4,'row'=2,'col'=4] {'leaf','row'}, dimensions={2}, use_global_device_ids=true | all-gather | bytes 110592 | tf_op jit(solution)/shard_map/all_gather | solution.py:194
  234.6 5.2 %all-gather = bf16[64,4,1,128]{3,0,1,2:T(8,128)(2,1)S(1)} all-gather(bf16[16,4,1,128]{3,0,1,2:T(8,128)(2,1)S(1)} %copy.196), channel_id=2, replica_groups=mesh['leaf'=4,'row'=2,'col'=4] {'col'}, dimensions={0}, use_global_device_ids=true | all-gather | bytes 81920 | tf_op jit(solution)/shard_map/all_gather | solution.py:210
  240.3 3.9 %collective-permute-done.9 = bf16[64,192]{1,0:T(8,128)(2,1)S(1)} collective-permute-done((bf16[64,192]{1,0:T(8,128)(2,1)S(1)}, bf16[64,192]{1,0:T(8,128)(2,1)S(1)}, u32[]{:S(2)}, u32[]{:S(2)}) %collective-permute-start.9) | collective-permute-done | bytes 24608 | tf_op jit(solution)/shard_map/ppermute | solution.py:22
  245.1 8.1 %reduce-scatter.15.cloned.1.call-done = bf16[96,64]{1,0:T(8,128)(2,1)} async-done(((bf16[192,64]{1,0:T(8,128)(2,1)}), bf16[96,64]{1,0:T(8,128)(2,1)}) %reduce-scatter.15.cloned.1.call-update) | async-done | bytes 12304
  254.0 5.2 %all-gather.2 = bf16[4,96,64]{1,2,0:T(8,128)(2,1)S(1)} all-gather(bf16[1,96,64]{1,2,0:T(8,128)(2,1)S(1)} %copy.170), channel_id=3, replica_groups=mesh['leaf'=4,'row'=2,'col'=4] {'col'}, dimensions={0}, use_global_device_ids=true | all-gather | bytes 61440 | tf_op jit(solution)/shard_map/all_gather | solution.py:217
  261.4 2.4 collective-permute-done.10
  264.7 10.0 %reduce-scatter.17.cloned.1.call-done = bf16[96,64]{1,0:T(8,128)(2,1)} async-done(((bf16[192,64]{1,0:T(8,128)(2,1)}), bf16[96,64]{1,0:T(8,128)(2,1)}) %reduce-scatter.17.cloned.1.call-update) | async-done | bytes 12304
  276.2 3.3 %all-to-all-start.3 = ((f32[64,1,96]{2,1,0:T(1,128)}), f32[64,1,96]{2,1,0:T(1,128)S(1)}, u32[]{:S(2)}, u32[]{:S(2)}) async-start(f32[64,1,96]{2,1,0:T(1,128)} %bitcast.55), calls=%async_computation.4 | async-start | bytes 65536 | tf_op jit(solution)/shard_map/all_to_all | solution.py:221
  279.4 3.9 %all-to-all-done.3 = f32[64,1,96]{2,1,0:T(1,128)S(1)} async-done(((f32[64,1,96]{2,1,0:T(1,128)}), f32[64,1,96]{2,1,0:T(1,128)S(1)}, u32[]{:S(2)}, u32[]{:S(2)}) %all-to-all-start.3) | async-done | bytes 24608 | tf_op jit(solution)/shard_map/all_to_all | solution.py:221
  283.5 5.3 %all_gather.23 = bf16[16,4,192]{0,1,2:T(4,128)(2,1)S(1)} all-gather(bf16[16,4,96]{0,1,2:T(4,128)(2,1)S(1)} %bitcast.187), channel_id=1, replica_groups=mesh['leaf'=4,'row'=2,'col'=4] {'row'}, dimensions={2}, use_global_device_ids=true | all-gather | bytes 36864 | tf_op jit(solution)/shard_map/all_gather | solution.py:26
  291.7 2.8 collective-permute-done.11
  (126 shorter events, 27.3 us)
Async XLA Ops:
  7.2 110.4 %copy-start = (bf16[4,96,768]{2,1,0:T(8,128)(2,1)S(1)}, bf16[4,96,768]{2,1,0:T(8,128)(2,1)}, u32[]{:S(2)}) copy-start(bf16[4,96,768]{2,1,0:T(8,128)(2,1)} %param.11) | copy-start | bytes 1769476
  7.2 1.0 copy-start.3
  17.7 11.7 %collective-permute-start = (bf16[16,4,448]{0,1,2:T(4,128)(2,1)S(1)}, bf16[16,4,448]{0,1,2:T(4,128)(2,1)S(1)}, u32[]{:S(2)}, u32[]{:S(2)}) collective-permute-start(bf16[16,4,448]{0,1,2:T(4,128)(2,1)S(1)} %all_gather.18), channel_id=1, source_target_pairs={{0,8},{8,0},{16,24},{24,16},{1,9},{9,1},{17,25},{25,17},{2,10},{10... | collective-permute-start | bytes 172040 | tf_op jit(solution)/shard_map/ppermute | solution.py:22
  19.8 0.7 copy-start.6
  30.6 8.1 %copy-start.2 = (bf16[4,96,384]{2,1,0:T(8,128)(2,1)S(1)}, bf16[4,96,384]{2,1,0:T(8,128)(2,1)}, u32[]{:S(2)}) copy-start(bf16[4,96,384]{2,1,0:T(8,128)(2,1)} %param.12) | copy-start | bytes 884740
  31.4 7.3 %all-to-all-start = ((bf16[16,4,384]{2,0,1:T(8,128)(2,1)}), bf16[16,4,384]{2,0,1:T(8,128)(2,1)S(1)}, u32[]{:S(2)}, u32[]{:S(2)}) async-start(bf16[16,4,384]{2,0,1:T(8,128)(2,1)} %bitcast.167), calls=%async_computation | async-start | bytes 98304 | tf_op jit(solution)/shard_map/all_to_all | solution.py:120
  34.7 46.6 %reduce-scatter.11.cloned.1.call-start = ((), (), s32[]{:S(2)}) async-start(), calls=%async_computation.8 | async-start | bytes 163840 | tf_op jit(solution)/shard_map/reduce_scatter | solution.py:132
  38.9 20.4 %copy-start.1 = (bf16[4,128,384]{2,1,0:T(8,128)(2,1)S(1)}, bf16[4,128,384]{2,1,0:T(8,128)(2,1)}, u32[]{:S(2)}) copy-start(bf16[4,128,384]{2,1,0:T(8,128)(2,1)} %param.13) | copy-start | bytes 1179652
  55.3 4.0 %collective-permute-start.1 = (bf16[64,1,192]{2,0,1:T(8,128)(2,1)S(1)}, bf16[64,1,192]{2,0,1:T(8,128)(2,1)S(1)}, u32[]{:S(2)}, u32[]{:S(2)}) collective-permute-start(bf16[64,1,192]{2,0,1:T(8,128)(2,1)S(1)} %copy.157), channel_id=1, source_target_pairs={{0,8},{8,0},{16,24},{24,16},{1,9},{9,1},{17,25},{25,17},{2,10},{10... | collective-permute-start | bytes 73736 | tf_op jit(solution)/shard_map/ppermute | solution.py:22
  60.2 0.7 copy-start.4
  60.2 132.7 %reduce-scatter.13.cloned.1.call-start = ((), (), s32[]{:S(2)}) async-start(), calls=%async_computation.9 | async-start | bytes 442368
  82.0 6.7 %collective-permute-start.2 = (bf16[16,4,224]{2,0,1:T(8,128)(2,1)S(1)}, bf16[16,4,224]{2,0,1:T(8,128)(2,1)S(1)}, u32[]{:S(2)}, u32[]{:S(2)}) collective-permute-start(bf16[16,4,224]{2,0,1:T(8,128)(2,1)S(1)} %pad_maximum_fusion.2), channel_id=1, source_target_pairs={{0,4},{4,8},{8,12},{12,16},{16,20},{20,24},{24,28},{28,0},{1,5},{5... | collective-permute-start | bytes 86024 | tf_op jit(solution)/shard_map/ppermute | solution.py:148
  88.7 6.6 %collective-permute-start.3 = (bf16[16,4,224]{2,0,1:T(8,128)(2,1)S(1)}, bf16[16,4,224]{2,0,1:T(8,128)(2,1)S(1)}, u32[]{:S(2)}, u32[]{:S(2)}) collective-permute-start(bf16[16,4,224]{2,0,1:T(8,128)(2,1)S(1)} %collective-permute-done.2), channel_id=1, source_target_pairs={{0,4},{4,8},{8,12},{12,16},{16,20},{20,24},{24,28},{28,0},{1,5},{5... | collective-permute-start | bytes 86024 | tf_op jit(solution)/shard_map/ppermute | solution.py:148
  88.7 6.6 %collective-permute-start.6 = (bf16[16,4,224]{2,0,1:T(8,128)(2,1)S(1)}, bf16[16,4,224]{2,0,1:T(8,128)(2,1)S(1)}, u32[]{:S(2)}, u32[]{:S(2)}) collective-permute-start(bf16[16,4,224]{2,0,1:T(8,128)(2,1)S(1)} %pad_maximum_fusion.2), channel_id=1, source_target_pairs={{4,0},{8,4},{12,8},{16,12},{20,16},{24,20},{28,24},{0,28},{5,1},{9... | collective-permute-start | bytes 86024 | tf_op jit(solution)/shard_map/ppermute | solution.py:151
  95.3 6.6 %collective-permute-start.4 = (bf16[16,4,224]{2,0,1:T(8,128)(2,1)S(1)}, bf16[16,4,224]{2,0,1:T(8,128)(2,1)S(1)}, u32[]{:S(2)}, u32[]{:S(2)}) collective-permute-start(bf16[16,4,224]{2,0,1:T(8,128)(2,1)S(1)} %collective-permute-done.3), channel_id=1, source_target_pairs={{0,4},{4,8},{8,12},{12,16},{16,20},{20,24},{24,28},{28,0},{1,5},{5... | collective-permute-start | bytes 86024 | tf_op jit(solution)/shard_map/ppermute | solution.py:148
  95.4 6.6 %collective-permute-start.7 = (bf16[16,4,224]{2,0,1:T(8,128)(2,1)S(1)}, bf16[16,4,224]{2,0,1:T(8,128)(2,1)S(1)}, u32[]{:S(2)}, u32[]{:S(2)}) collective-permute-start(bf16[16,4,224]{2,0,1:T(8,128)(2,1)S(1)} %collective-permute-done.6), channel_id=1, source_target_pairs={{4,0},{8,4},{12,8},{16,12},{20,16},{24,20},{28,24},{0,28},{5,1},{9... | collective-permute-start | bytes 86024 | tf_op jit(solution)/shard_map/ppermute | solution.py:151
  102.0 6.6 %collective-permute-start.5 = (bf16[16,4,224]{2,0,1:T(8,128)(2,1)S(1)}, bf16[16,4,224]{2,0,1:T(8,128)(2,1)S(1)}, u32[]{:S(2)}, u32[]{:S(2)}) collective-permute-start(bf16[16,4,224]{2,0,1:T(8,128)(2,1)S(1)} %collective-permute-done.4), channel_id=1, source_target_pairs={{0,4},{4,8},{8,12},{12,16},{16,20},{20,24},{24,28},{28,0},{1,5},{5... | collective-permute-start | bytes 86024 | tf_op jit(solution)/shard_map/ppermute | solution.py:148
  102.0 6.7 %collective-permute-start.8 = (bf16[16,4,224]{2,0,1:T(8,128)(2,1)S(1)}, bf16[16,4,224]{2,0,1:T(8,128)(2,1)S(1)}, u32[]{:S(2)}, u32[]{:S(2)}) collective-permute-start(bf16[16,4,224]{2,0,1:T(8,128)(2,1)S(1)} %collective-permute-done.7), channel_id=1, source_target_pairs={{4,0},{8,4},{12,8},{16,12},{20,16},{24,20},{28,24},{0,28},{5,1},{9... | collective-permute-start | bytes 86024 | tf_op jit(solution)/shard_map/ppermute | solution.py:151
  109.5 0.7 copy-start.5
  194.4 7.2 %all-to-all-start.2 = ((f32[64,1,96]{2,1,0:T(1,128)}), f32[64,1,96]{2,1,0:T(1,128)S(1)}, u32[]{:S(2)}, u32[]{:S(2)}) async-start(f32[64,1,96]{2,1,0:T(1,128)} %bitcast.37), calls=%async_computation.3 | async-start | bytes 65536 | tf_op jit(solution)/shard_map/all_to_all | solution.py:187
  197.7 55.5 %reduce-scatter.15.cloned.1.call-start = ((), (), s32[]{:S(2)}) async-start(), calls=%async_computation.10 | async-start | bytes 73728
  240.2 4.0 %collective-permute-start.9 = (bf16[64,192]{1,0:T(8,128)(2,1)S(1)}, bf16[64,192]{1,0:T(8,128)(2,1)S(1)}, u32[]{:S(2)}, u32[]{:S(2)}) collective-permute-start(bf16[64,192]{1,0:T(8,128)(2,1)S(1)} %select_convert_fusion.1), channel_id=1, source_target_pairs={{0,8},{8,0},{16,24},{24,16},{1,9},{9,1},{17,25},{25,17},{2,10},{10... | collective-permute-start | bytes 73736 | tf_op jit(solution)/shard_map/ppermute | solution.py:22
  245.0 29.7 %reduce-scatter.17.cloned.1.call-start = ((), (), s32[]{:S(2)}) async-start(), calls=%async_computation.11 | async-start | bytes 73728
  259.9 4.0 %collective-permute-start.10 = (bf16[64,192]{1,0:T(8,128)(2,1)S(1)}, bf16[64,192]{1,0:T(8,128)(2,1)S(1)}, u32[]{:S(2)}, u32[]{:S(2)}) collective-permute-start(bf16[64,192]{1,0:T(8,128)(2,1)S(1)} %select_convert_fusion), channel_id=1, source_target_pairs={{0,8},{8,0},{16,24},{24,16},{1,9},{9,1},{17,25},{25,17},{2,10},{10... | collective-permute-start | bytes 73736 | tf_op jit(solution)/shard_map/ppermute | solution.py:22
  276.2 7.2 %all-to-all-start.3 = ((f32[64,1,96]{2,1,0:T(1,128)}), f32[64,1,96]{2,1,0:T(1,128)S(1)}, u32[]{:S(2)}, u32[]{:S(2)}) async-start(f32[64,1,96]{2,1,0:T(1,128)} %bitcast.55), calls=%async_computation.4 | async-start | bytes 65536 | tf_op jit(solution)/shard_map/all_to_all | solution.py:221
  288.8 5.7 %collective-permute-start.11 = (bf16[16,4,192]{0,1,2:T(4,128)(2,1)S(1)}, bf16[16,4,192]{0,1,2:T(4,128)(2,1)S(1)}, u32[]{:S(2)}, u32[]{:S(2)}) collective-permute-start(bf16[16,4,192]{0,1,2:T(4,128)(2,1)S(1)} %all_gather.23), channel_id=1, source_target_pairs={{0,8},{8,0},{16,24},{24,16},{1,9},{9,1},{17,25},{25,17},{2,10},{10... | collective-permute-start | bytes 73736 | tf_op jit(solution)/shard_map/ppermute | solution.py:22
Sparse Core Ops, SparseCore 0:
  60.4 20.8 reduce-scatter.10
  130.3 62.5 reduce-scatter.12
  245.1 8.0 reduce-scatter.14
  264.8 9.8 reduce-scatter.16
